TPU v7x, 256 devices: a whole 4x4x8 slice. The times are simulated.
256 devices in a mesh: seq: 32 (over y, z), head: 8 (over x, core).
Axes of the slice: x: 4, y: 4, z: 8, core: 2. Of those that a mesh axis runs over, the one named last changes fastest.
Arguments:
- hidden: bfloat16 [16384, 8192], P('seq', 'head'), may hold values from -6 to 6
- gain: float32 [8192], replicated, may hold values from 0.25 to 1.75
- key_matrix: bfloat16 [8192, 1024], P(None, 'head'), may hold values from -0.0625 to 0.0625
- value_matrix: bfloat16 [8192, 1024], P(None, 'head'), may hold values from -0.0625 to 0.0625
- queries: bfloat16 [64, 8192], P(None, 'head'), may hold values from -360 to 360
- window_len: int32 [8], P('head'), may hold values from 16 to 64, as said below
- kernel_width: int32 [8], P('head'), may hold values from 1 to 15, as said below
- kept_block_count: int32 [8], P('head'), may hold values from 1 to 64
Outputs:
- block_scores: float32 [8, 128], P('head', 'seq')
- kept_fraction: float32 [8], P('head')
Inputs may be any that keep to these rules, and one draw needn't show every extreme that they name: `window_len`: at least one key-value head uses all 64 window queries. `kernel_width`: odd; at least one key-value head has width 15.
All inputs are finite; a program needn't handle non-finite values.
Results may differ from a plain program's by a relative error of at most 0.0112.
The roundings to bfloat16 on the way count: a program that leaves them out, or rounds other values in their place, can miss the bound.
Values may be sent and summed in bfloat16 or wider, within the bound.
A program may use at most 128 MiB of HBM per device.

v0:
```python
import jax
import jax.numpy as jnp
from jax import lax
from jax.sharding import PartitionSpec as P

BLK = 128
KERNEL_LIMIT = 15


def copy_for_each(x, axis):
    count = lax.axis_size(axis)
    return lax.all_to_all(jnp.broadcast_to(x[None], (count, *x.shape)), axis, 0, 0, tiled=True)


def taken_together(x, axis):
    return copy_for_each(x, axis).sum(axis=0)


def gathered_once(x, axis):
    leaves = jax.tree.leaves(x)
    order = sorted(range(len(leaves)), key=lambda k: -leaves[k].size)
    width = (1, *leaves[order[0]].shape)[-1]
    lines = [
        jnp.pad(leaves[k].reshape(-1), (0, -leaves[k].size % width)).reshape(-1, width)
        for k in order
    ]
    both, at, found = (copy_for_each(jnp.concatenate(lines), axis), 0, {})
    for k, line in zip(order, lines):
        section = both[:, at : at + len(line)].reshape(len(both), -1)
        found[k] = section[:, : leaves[k].size].reshape(-1, *leaves[k].shape)
        at += len(line)
    numbers = iter(range(len(leaves)))
    return jax.tree.map(lambda _: found[next(numbers)], x)


def combined_pairwise(pieces, combine):
    while len(jax.tree.leaves(pieces)[0]) > 1:
        pieces = jax.vmap(combine)(
            *(jax.tree.map(lambda part: part[side::2], pieces) for side in (0, 1))
        )
    return jax.tree.map(lambda part: part[0], pieces)


def joined_all(x, axis, combine):
    pieces = gathered_once(x, axis)
    return combined_pairwise(pieces, combine)


def with_halo(x, sides, width):
    for axis, dim in sides:
        count, length = (lax.axis_size(axis), x.shape[dim])
        up = [(i, (i + 1) % count) for i in range(count - 1)]
        down = [(j, i) for i, j in up]
        last = lax.slice_in_dim(x, length - width, length, axis=dim)
        leading = lax.slice_in_dim(x, 0, width, axis=dim)
        before = lax.ppermute(last, axis, up)
        after = lax.ppermute(leading, axis, down)
        x = jnp.concatenate([before, x, after], axis=dim)
    return x


def laid_out(tiles, dim):
    lengths = list(tiles.shape[1:])
    lengths[dim] *= tiles.shape[0]
    return jnp.moveaxis(tiles, 0, dim).reshape(lengths)


def gathered_copies(x, axis, dim):
    return laid_out(copy_for_each(x, axis), dim)


def rotate(raw, positions):
    half = raw.shape[1] // 2
    freq = 500000.0 ** (-(jnp.arange(half).astype(jnp.float32) * 2.0) / raw.shape[1])
    angle = positions[:, None] * freq[None, :]
    leading_part = raw[:, :half]
    trailing_part = raw[:, half:]
    return jnp.concatenate(
        [
            leading_part * jnp.cos(angle) - trailing_part * jnp.sin(angle),
            trailing_part * jnp.cos(angle) + leading_part * jnp.sin(angle),
        ],
        axis=1,
    )


def combine_stats(earlier, later):
    top = jnp.maximum(earlier[0], later[0])
    total = earlier[1] * jnp.exp(earlier[0] - top) + later[1] * jnp.exp(later[0] - top)
    return (top, total)


def local(
    hidden, gain, key_matrix, value_matrix, queries, window_len, kernel_width, kept_block_count
):
    tok_rows = hidden.shape[0]
    full_width = gain.shape[0]
    head_size = key_matrix.shape[1]
    floats = hidden.astype(jnp.float32)
    sumsq = taken_together(jnp.sum(floats * floats, axis=1), "head")
    inv_rms = lax.rsqrt(sumsq / full_width + 1e-05)
    joined = jnp.concatenate([key_matrix, value_matrix], axis=1)
    normed = (
        lax.all_gather(hidden, "head", axis=1, tiled=True).astype(jnp.float32) * gain[None, :]
    ).astype(jnp.bfloat16)
    projected = jnp.dot(normed, joined, preferred_element_type=jnp.float32)
    projected = projected * inv_rms[:, None]
    tok_index = lax.axis_index("seq") * tok_rows + jnp.arange(tok_rows)
    positions = tok_index.astype(jnp.float32)
    keys = rotate(projected[:, :head_size], positions).astype(jnp.bfloat16)
    vmag = jnp.mean(jnp.abs(projected[:, head_size:]), axis=1)
    window = queries.shape[0]
    group_heads = queries.shape[1] // head_size
    query_rows = queries.reshape(window * group_heads, head_size)
    scores = lax.dot_general(
        query_rows, keys, (((1,), (1,)), ((), ())), preferred_element_type=jnp.float32
    ) * head_size ** (-0.5)
    total_tokens = tok_rows * lax.axis_size("seq")
    limit = jnp.repeat(total_tokens - window + jnp.arange(window), group_heads)
    allowed = tok_index[None, :] <= limit[:, None]
    scores = jnp.where(allowed, scores, jnp.float32(-1e30))
    local_top = jnp.max(scores, axis=1)
    local_expo = jnp.exp(scores - local_top[:, None])
    local_total = jnp.sum(local_expo, axis=1)
    row_top, row_total = joined_all((local_top, local_total), "seq", combine_stats)
    rescale = jnp.exp(local_top - row_top)
    used = (jnp.arange(window) >= window - window_len[0]).astype(jnp.float32)
    row_weight = jnp.repeat(used, group_heads) * rescale / row_total
    column = jnp.dot(row_weight, local_expo, precision=lax.Precision.HIGHEST) * vmag
    reach = (KERNEL_LIMIT - 1) // 2
    padded = with_halo(column, (("seq", 0),), reach)
    kernel_halfspan = (kernel_width[0] - 1) // 2
    pooled = column
    for shift in range(1, reach + 1):
        wider = jnp.maximum(
            jnp.maximum(pooled, padded[reach + shift : reach + shift + tok_rows]),
            padded[reach - shift : reach - shift + tok_rows],
        )
        pooled = jnp.where(shift <= kernel_halfspan, wider, pooled)
    local_blocks = jnp.sum(pooled.reshape(tok_rows // BLK, BLK), axis=1)[None, :]
    everything = gathered_copies(local_blocks, "seq", 1)[0]
    ordered = -jnp.sort(-everything)
    ranks = jnp.arange(ordered.shape[0])
    kept = jnp.sum(jnp.where(ranks < kept_block_count[0], ordered, jnp.float32(0.0)))
    fraction = (kept / jnp.sum(ordered)).reshape(1)
    return (local_blocks, fraction)


def solution(mesh):
    return jax.shard_map(
        local,
        mesh=mesh,
        in_specs=(
            P("seq", "head"),
            P(),
            P(None, "head"),
            P(None, "head"),
            P(None, "head"),
            P("head"),
            P("head"),
            P("head"),
        ),
        out_specs=(P("head", "seq"), P("head")),
        check_vma=False,
    )
```

profile of v0, /device:TPU:1, one launch (start us, length us, event | category | flops | bytes accessed | tf_op | source)
XLA Modules:
  0.0 131.5 jit_solution(4325078742741071064)
XLA Ops:
  7.2 0.7 all-gather.2.cloned.1.call-update
  7.9 1.5 %multiply_reduce_fusion = f32[512]{0:T(512)S(1)} fusion(bf16[512,1024]{1,0:T(8,128)(2,1)} %param.8), kind=kLoop, calls=%fused_computation.6 | loop fusion | flops 1572352 | bytes 1050624 | tf_op jit(solution)/shard_map/reduce_sum | solution.py:100
  9.4 0.6 broadcast_in_dim.21
  10.0 6.4 %all-to-all-start = ((f32[8,1,512]{2,1,0:T(1,128)}), f32[8,1,512]{2,1,0:T(1,128)S(1)}, u32[]{:S(2)}, u32[]{:S(2)}) async-start(f32[8,1,512]{2,1,0:T(1,128)} %broadcast_in_dim.21), calls=%async_computation | async-start | bytes 32768 | tf_op jit(solution)/shard_map/all_to_all | solution.py:12
  16.5 1.0 reshape.69
  17.6 3.5 %all-to-all-done = f32[8,1,512]{2,1,0:T(1,128)S(1)} async-done(((f32[8,1,512]{2,1,0:T(1,128)}), f32[8,1,512]{2,1,0:T(1,128)S(1)}, u32[]{:S(2)}, u32[]{:S(2)}) %all-to-all-start) | async-done | bytes 16416 | tf_op jit(solution)/shard_map/all_to_all | solution.py:12
  21.1 45.1 %all-gather.2.cloned.1.call-done = bf16[512,8192]{1,0:T(8,128)(2,1)} async-done(((bf16[512,1024]{1,0:T(8,128)(2,1)}), bf16[512,8192]{1,0:T(8,128)(2,1)}) %all-gather.2.cloned.1.call-update) | async-done | bytes 8388624 | tf_op jit(solution)/shard_map/all_gather | solution.py:104
  66.2 7.0 %fusion.7 = f32[512,256]{0,1:T(8,128)S(1)} fusion(bf16[8192,128]{1,0:T(8,128)(2,1)} %param.11, bf16[8192,128]{1,0:T(8,128)(2,1)} %param.10, bf16[512,8192]{1,0:T(8,128)(2,1)} %all-gather.2.cloned.1.call-done, f32[8192]{0:T(1024)} %param.9, f32[512]{0:T(512)S(1)} %add_rsqrt_fusion), kind=kOutput, calls=%fused_computation.10 | convolution fusion | flops 2168586240 | bytes 13142016 | tf_op jit(solution)/shard_map/dot_general | solution.py:106
  73.2 0.6 fusion.19
  73.8 0.4 fusion.33
  74.1 0.2 fusion.11
  74.3 0.7 broadcast_in_dim.44
  75.0 9.6 %all-to-all-start.1 = ((f32[32,2,512]{2,1,0:T(2,128)}), f32[32,2,512]{2,1,0:T(2,128)S(1)}, u32[]{:S(2)}, u32[]{:S(2)}) async-start(f32[32,2,512]{2,1,0:T(2,128)} %broadcast_in_dim.44), calls=%async_computation.1 | async-start | bytes 262144 | tf_op jit(solution)/shard_map/all_to_all | solution.py:12
  86.1 7.6 %all-to-all-done.1 = f32[32,2,512]{2,1,0:T(2,128)S(1)} async-done(((f32[32,2,512]{2,1,0:T(2,128)}), f32[32,2,512]{2,1,0:T(2,128)S(1)}, u32[]{:S(2)}, u32[]{:S(2)}) %all-to-all-start.1) | async-done | bytes 131104 | tf_op jit(solution)/shard_map/all_to_all | solution.py:12
  94.3 1.0 fusion.10
  95.4 1.3 collective-permute-start
  96.7 4.1 %collective-permute-start.1 = (f32[7]{0:T(128)S(1)}, f32[7]{0:T(128)S(1)}, u32[]{:S(2)}, u32[]{:S(2)}) collective-permute-start(f32[7]{0:T(128)S(1)} %get-tuple-element.24), channel_id=1, source_target_pairs={{0,8},{8,16},{16,24},{24,32},{32,40},{40,48},{48,56},{56,64},{64,7... | collective-permute-start | bytes 92 | tf_op jit(solution)/shard_map/ppermute | solution.py:56
  100.8 0.7 collective-permute-done.1
  101.6 0.2 bitcast_reduce_fusion
  101.8 0.6 broadcast_in_dim.46
  102.4 7.7 %all-to-all-start.2 = ((f32[32,1,4]{2,1,0:T(1,128)}), f32[32,1,4]{2,1,0:T(1,128)S(1)}, u32[]{:S(2)}, u32[]{:S(2)}) async-start(f32[32,1,4]{2,1,0:T(1,128)} %broadcast_in_dim.46), calls=%async_computation.2 | async-start | bytes 32768 | tf_op jit(solution)/shard_map/all_to_all | solution.py:12
  110.7 8.0 %all-to-all-done.2 = f32[32,1,4]{2,1,0:T(1,128)S(1)} async-done(((f32[32,1,4]{2,1,0:T(1,128)}), f32[32,1,4]{2,1,0:T(1,128)S(1)}, u32[]{:S(2)}, u32[]{:S(2)}) %all-to-all-start.2) | async-done | bytes 544 | tf_op jit(solution)/shard_map/all_to_all | solution.py:12
  118.9 2.6 %sort.15 = (f32[128]{0:T(128)S(1)}, s32[128]{0:T(128)}) sort(f32[128]{0:T(128)S(1)} %neg.20, s32[128]{0:T(128)S(1)} %iota.29), dimensions={0}, to_apply=%region_6.7 | sort | flops 896 | bytes 2048 | tf_op jit(solution)/shard_map/jit(sort)/sort | solution.py:142
  121.5 0.7 fusion.30
  (47 shorter events, 1.3 us)
Async XLA Ops:
  7.2 59.1 %all-gather.2.cloned.1.call-start = ((), (), s32[]{:S(2)}) async-start(), calls=%async_computation.3 | async-start | bytes 9437184 | tf_op jit(solution)/shard_map/all_gather | solution.py:104
  10.0 11.1 %all-to-all-start = ((f32[8,1,512]{2,1,0:T(1,128)}), f32[8,1,512]{2,1,0:T(1,128)S(1)}, u32[]{:S(2)}, u32[]{:S(2)}) async-start(f32[8,1,512]{2,1,0:T(1,128)} %broadcast_in_dim.21), calls=%async_computation | async-start | bytes 32768 | tf_op jit(solution)/shard_map/all_to_all | solution.py:12
  75.0 18.7 %all-to-all-start.1 = ((f32[32,2,512]{2,1,0:T(2,128)}), f32[32,2,512]{2,1,0:T(2,128)S(1)}, u32[]{:S(2)}, u32[]{:S(2)}) async-start(f32[32,2,512]{2,1,0:T(2,128)} %broadcast_in_dim.44), calls=%async_computation.1 | async-start | bytes 262144 | tf_op jit(solution)/shard_map/all_to_all | solution.py:12
  95.4 5.4 %collective-permute-start = (f32[7]{0:T(128)S(1)}, f32[7]{0:T(128)S(1)}, u32[]{:S(2)}, u32[]{:S(2)}) collective-permute-start(f32[7]{0:T(128)S(1)} %get-tuple-element.23), channel_id=1, source_target_pairs={{8,0},{16,8},{24,16},{32,24},{40,32},{48,40},{56,48},{64,56},{72,6... | collective-permute-start | bytes 92 | tf_op jit(solution)/shard_map/ppermute | solution.py:57
  96.7 4.8 %collective-permute-start.1 = (f32[7]{0:T(128)S(1)}, f32[7]{0:T(128)S(1)}, u32[]{:S(2)}, u32[]{:S(2)}) collective-permute-start(f32[7]{0:T(128)S(1)} %get-tuple-element.24), channel_id=1, source_target_pairs={{0,8},{8,16},{16,24},{24,32},{32,40},{40,48},{48,56},{56,64},{64,7... | collective-permute-start | bytes 92 | tf_op jit(solution)/shard_map/ppermute | solution.py:56
  101.8 21.7 %copy-start = (f32[4]{0:T(128)}, f32[4]{0:T(128)S(1)}, u32[]{:S(2)}) copy-start(f32[4]{0:T(128)S(1)} %bitcast_reduce_fusion) | copy-start | bytes 52
  102.4 16.3 %all-to-all-start.2 = ((f32[32,1,4]{2,1,0:T(1,128)}), f32[32,1,4]{2,1,0:T(1,128)S(1)}, u32[]{:S(2)}, u32[]{:S(2)}) async-start(f32[32,1,4]{2,1,0:T(1,128)} %broadcast_in_dim.46), calls=%async_computation.2 | async-start | bytes 32768 | tf_op jit(solution)/shard_map/all_to_all | solution.py:12
Sparse Core Ops, SparseCore 0:
  9.8 56.3 all-gather.1
where the time goes:
time: 134 us; the launch traced here: 132 us
  waiting for transfers between devices  65.5 us (49%)
  starting transfers between devices  29.1 us (22%)
  between operations  18.7 us (14%)
  matrix products  8.29 us (6%)
  other arithmetic  6.1 us (5%)
  local copies, waits for them, and re-layouts  3.82 us (3%)
    all_gather x1, waiting for transfers between devices, local(): lax.all_gather(hidden, 'head', axis=1, tiled=True).astype(jnp.float32)  45.1 us
    all_to_all x3, starting transfers between devices, copy_for_each(): lax.all_to_all(jnp.broadcast_to(x[None], (count, *x.shape)), axis, 0, 0,...  23.7 us
    all_to_all x3, waiting for transfers between devices, copy_for_each(): lax.all_to_all(jnp.broadcast_to(x[None], (count, *x.shape)), axis, 0, 0,...  19.1 us
    dot_general x1, matrix products, local(): projected = jnp.dot(normed, joined, preferred_element_type=jnp.float32)  6.96 us
    ppermute x1, starting transfers between devices, with_halo(): before = lax.ppermute(last, axis, up)  4.1 us
  transfers between devices with their start and end apart: 6, of which 5 were waited for; matrix products, arithmetic and copies ran while one was open for 3% of the time, Pallas kernels for 0%

commit v1 on v0

v1 whole, which is shorter than its diff:
```python
import functools

import jax
import jax.numpy as jnp
import numpy as np
from jax import lax
from jax.experimental import pallas as pl
from jax.experimental.pallas import tpu as pltpu
from jax.sharding import PartitionSpec as P

MESH = pl.DeviceIdType.MESH
BLK = 128
KERNEL_LIMIT = 15
NX = 4
CHUNKS = 8
NEG = -1e30


def kernel(
    n_seq,
    hid, gain, wk, wv, q, wlen, kwidth, keep, freq,
    blocks_out, frac_out,
    hbuf, w, qs, cos_t, sin_t, acc, ssq, vmag, ex, stat, gt, ext, halo_p,
    halo_send, halo_recv, stat_recv, blk_recv,
    load_sem, own_send, fwd_send, d2d_own_send, d2d_send, recv_sem,
    halo_ssem, halo_rsem, stat_ssem, stat_rsem, blk_ssem, blk_rsem,
):
    tok = hid.shape[0]
    feat = hid.shape[1]
    hd = wk.shape[1]
    window = q.shape[0]
    group = q.shape[1] // hd
    nq = window * group
    nb = tok // BLK
    rows = tok // CHUNKS
    half = CHUNKS // 2
    full_width = gain.shape[1]
    total_tokens = tok * n_seq

    s = lax.axis_index("seq")
    h = lax.axis_index("head")
    x, c = h // 2, lax.rem(h, 2)
    xr, xl, xo = lax.rem(x + 1, NX), lax.rem(x + 3, NX), lax.rem(x + 2, NX)
    right = {"seq": s, "head": xr * 2 + c}
    left = {"seq": s, "head": xl * 2 + c}
    partner = {"seq": s, "head": x * 2 + 1 - c}
    seq_next = {"seq": lax.rem(s + 1, n_seq), "head": h}
    seq_prev = {"seq": lax.rem(s + n_seq - 1, n_seq), "head": h}

    src = [x * 2 + c, xl * 2 + c, xr * 2 + c, xo * 2 + c]
    src += [x * 2 + 1 - c, xl * 2 + 1 - c, xr * 2 + 1 - c, xo * 2 + 1 - c]

    loads = [
        pltpu.make_async_copy(hid, hbuf.at[0], load_sem.at[0]),
        pltpu.make_async_copy(wk, w.at[:, 0:hd], load_sem.at[1]),
        pltpu.make_async_copy(wv, w.at[:, hd : 2 * hd], load_sem.at[2]),
    ]
    for cp in loads:
        cp.start()

    barrier = pltpu.get_barrier_semaphore()
    for dev in (right, left, partner):
        pl.semaphore_signal(barrier, inc=1, device_id=dev, device_id_type=MESH)

    def greet(d, carry):
        dev = {"seq": lax.rem(s + d, n_seq), "head": h}
        pl.semaphore_signal(barrier, inc=1, device_id=dev, device_id_type=MESH)
        return carry

    lax.fori_loop(1, n_seq, greet, 0)
    pl.semaphore_wait(barrier, 3 + n_seq - 1)

    def part(k):
        return slice(k * rows, (k + 1) * rows)

    def send(source, slot, k, ssem, dev):
        return pltpu.make_async_remote_copy(
            src_ref=source, dst_ref=hbuf.at[slot, part(k)], send_sem=ssem,
            recv_sem=recv_sem.at[slot, k], device_id=dev, device_id_type=MESH,
        )

    started = []

    def go(cp):
        cp.start()
        started.append(cp)

    for k in range(CHUNKS):
        go(send(hid.at[part(k)], 1, k, own_send.at[0, k], right))
        go(send(hid.at[part(k)], 2, k, own_send.at[1, k], left))
    for k in range(CHUNKS):
        go(send(hid.at[part(k)], 4, k, d2d_own_send.at[k], partner))

    def landed(slot, k):
        send(hbuf.at[slot, part(k)], slot, k, own_send.at[0, 0], right).wait_recv()

    for b in range(nb):
        position = (s * tok + b * BLK + lax.broadcasted_iota(jnp.int32, (BLK, hd), 0)).astype(jnp.float32)
        angle = position * freq[0:1, :]
        lane = lax.broadcasted_iota(jnp.int32, (BLK, hd), 1)
        cos_t[b * BLK : (b + 1) * BLK, :] = jnp.cos(angle)
        sine = jnp.sin(angle)
        sin_t[b * BLK : (b + 1) * BLK, :] = jnp.where(lane < hd // 2, -sine, sine)
    for j in range(group):
        qs[j * window : (j + 1) * window, :] = q[:, j * hd : (j + 1) * hd]
    for cp in loads:
        cp.wait()

    def accumulate(slot, first, count, size, fresh=False):
        head = src[slot]
        offset = pl.multiple_of(head * feat, feat)

        def body(i, carry):
            at = pl.ds(pl.multiple_of(first + i * size, size), size)
            block = hbuf[slot, at, :].astype(jnp.float32)
            normed = (block * gain[0:1, pl.ds(offset, feat)]).astype(jnp.bfloat16)
            product = jnp.dot(normed, w[pl.ds(offset, feat), :], preferred_element_type=jnp.float32)
            square = block * block
            lanes = square[:, 0:128]
            for t in range(1, feat // 128):
                lanes = lanes + square[:, t * 128 : (t + 1) * 128]
            if fresh:
                acc[at, :] = product
                ssq[at, :] = lanes
            else:
                acc[at, :] += product
                ssq[at, :] += lanes
            return carry

        lax.fori_loop(0, count, body, 0)

    accumulate(0, 0, nb, BLK, fresh=True)
    for k in range(CHUNKS):
        landed(4, k)
    accumulate(4, 0, nb, BLK)

    per = BLK // rows
    for b in range(nb):
        for k in range(b * per, (b + 1) * per):
            landed(1, k)
            if k < half:
                go(send(hbuf.at[1, part(k)], 3, k, fwd_send.at[k], right))
            go(send(hbuf.at[1, part(k)], 5, k, d2d_send.at[0, k], partner))
            landed(2, k)
            if k >= half:
                go(send(hbuf.at[2, part(k)], 3, k, fwd_send.at[k], left))
            go(send(hbuf.at[2, part(k)], 6, k, d2d_send.at[1, k], partner))
        accumulate(1, b * BLK, 1, BLK)
        accumulate(2, b * BLK, 1, BLK)
        for k in range(b * per, (b + 1) * per):
            landed(5, k)
            landed(6, k)
        accumulate(5, b * BLK, 1, BLK)
        accumulate(6, b * BLK, 1, BLK)

    lane_q = lax.broadcasted_iota(jnp.int32, (1, nq), 1)
    limit = total_tokens - window + lax.rem(lane_q, window)

    def scores_of(keys):
        return lax.dot_general(
            keys, qs[...], (((1,), (1,)), ((), ())), preferred_element_type=jnp.float32
        ) * hd ** (-0.5)

    def halo_copy(side, dev):
        return pltpu.make_async_remote_copy(
            src_ref=halo_send.at[side], dst_ref=halo_recv.at[side], send_sem=halo_ssem.at[side],
            recv_sem=halo_rsem.at[side], device_id=dev, device_id_type=MESH,
        )

    def finish(b):
        at = slice(b * BLK, (b + 1) * BLK)
        meansq = jnp.sum(ssq[at, :], axis=1, keepdims=True) / full_width
        inv = lax.rsqrt(meansq + 1e-05)
        kraw = acc[at, 0:hd] * inv
        vraw = acc[at, hd : 2 * hd] * inv
        keys = (kraw * cos_t[at, :] + pltpu.roll(kraw, hd // 2, 1) * sin_t[at, :]).astype(jnp.bfloat16)
        mag = jnp.sum(jnp.abs(vraw), axis=1, keepdims=True) / hd
        mag = jnp.broadcast_to(mag, (BLK, 128))
        vmag[at, :] = mag
        if b == 0:
            halo_send[0, 0] = keys[0:16, :].astype(jnp.float32)
            halo_send[0, 1] = mag[0:16, :]
            go(halo_copy(0, seq_prev))
        if b == nb - 1:
            halo_send[1, 0] = keys[BLK - 16 :, :].astype(jnp.float32)
            halo_send[1, 1] = mag[BLK - 16 :, :]
            go(halo_copy(1, seq_next))
        scores = scores_of(keys)
        token = s * tok + b * BLK + lax.broadcasted_iota(jnp.int32, (BLK, nq), 0)
        scores = jnp.where(token <= limit, scores, NEG)
        top = jnp.max(scores, axis=0, keepdims=True)
        expo = jnp.exp(scores - top)
        ex[at, :] = expo
        tot = jnp.sum(expo, axis=0, keepdims=True)
        for j in range(nq // 128):
            stat[b, j : j + 1, :] = top[:, j * 128 : (j + 1) * 128]
            stat[b, 4 + j : 5 + j, :] = tot[:, j * 128 : (j + 1) * 128]

    for k in range(half):
        landed(3, k)
        go(send(hbuf.at[3, part(k)], 7, k, d2d_send.at[2, k], partner))
        landed(3, half + k)
        go(send(hbuf.at[3, part(half + k)], 7, half + k, d2d_send.at[2, half + k], partner))
        if (k + 1) % per == 0:
            i = k // per
            for b in (i, nb // 2 + i):
                accumulate(3, b * BLK, 1, BLK)
                for m in range(b * per, (b + 1) * per):
                    landed(7, m)
                accumulate(7, b * BLK, 1, BLK)
                finish(b)

    merged = stat[0]
    for b in range(1, nb):
        other = stat[b]
        top = jnp.maximum(merged, other)
        scaled = pltpu.roll(jnp.exp(merged - top), 4, 0) * merged + pltpu.roll(jnp.exp(other - top), 4, 0) * other
        sub = lax.broadcasted_iota(jnp.int32, (8, 128), 0)
        merged = jnp.where(sub < 4, top, scaled)
    stat_recv[s] = merged

    def stat_copy(d):
        return pltpu.make_async_remote_copy(
            src_ref=stat_recv.at[s], dst_ref=stat_recv.at[s], send_sem=stat_ssem.at[d],
            recv_sem=stat_rsem.at[d], device_id={"seq": lax.rem(s + d, n_seq), "head": h}, device_id_type=MESH,
        )

    def blk_copy(d):
        return pltpu.make_async_remote_copy(
            src_ref=blk_recv.at[s], dst_ref=blk_recv.at[s], send_sem=blk_ssem.at[d],
            recv_sem=blk_rsem.at[d], device_id={"seq": lax.rem(s + d, n_seq), "head": h}, device_id_type=MESH,
        )

    def each_peer(act):
        def body(d, carry):
            act(d)
            return carry

        lax.fori_loop(1, n_seq, body, 0)

    each_peer(lambda d: stat_copy(d).start())

    halo_copy(0, seq_prev).wait_recv()
    halo_copy(1, seq_next).wait_recv()
    edge_keys = jnp.concatenate([halo_recv[0, 0], halo_recv[1, 0]], axis=0).astype(jnp.bfloat16)
    edge_scores = scores_of(edge_keys)
    edge_row = lax.broadcasted_iota(jnp.int32, (32, nq), 0)
    edge_token = jnp.where(edge_row < 16, (s + 1) * tok + edge_row, s * tok - 32 + edge_row)
    edge_ok = (edge_token >= 0) & (edge_token <= limit)
    edge_scores = jnp.where(edge_ok, edge_scores, NEG)
    edge_top = jnp.max(edge_scores, axis=0, keepdims=True)
    edge_expo = jnp.where(edge_ok, jnp.exp(edge_scores - edge_top), 0.0)
    for j in range(nq // 128):
        stat[nb, j : j + 1, :] = edge_top[:, j * 128 : (j + 1) * 128]

    each_peer(lambda d: stat_copy(d).wait_recv())
    everyone = stat_recv[...]
    row_top = jnp.max(everyone, axis=0)
    row_total = jnp.sum(pltpu.roll(jnp.exp(everyone - row_top[None]), 4, 1) * everyone, axis=0)
    row_total = pltpu.roll(row_total, 4, 0)
    sub8 = lax.broadcasted_iota(jnp.int32, (8, 128), 0)
    lane8 = lax.broadcasted_iota(jnp.int32, (8, 128), 1)
    wrow = lax.rem(lane8, window)
    used = (wrow >= window - wlen[0]) & (sub8 < 4)
    for b in range(nb + 1):
        factor = jnp.exp(stat[b] - row_top) / row_total
        gt[b] = jnp.where(used, factor, 0.0)

    def weighted(expo, b):
        total = expo[:, 0:128] * gt[b, 0:1, :]
        for j in range(1, nq // 128):
            total = total + expo[:, j * 128 : (j + 1) * 128] * gt[b, j : j + 1, :]
        return total

    ext[...] = jnp.zeros_like(ext)
    for b in range(nb):
        at = slice(b * BLK, (b + 1) * BLK)
        column = weighted(ex[at, :], b) * vmag[at, :]
        ext[b + 1 : b + 2, :] = jnp.sum(column.T, axis=0, keepdims=True)
    edge = weighted(edge_expo, nb)
    halo_p[...] = jnp.zeros_like(halo_p)
    halo_p[0:16, :] = edge[0:16, :] * halo_recv[0, 1]
    halo_p[BLK - 16 :, :] = edge[16:32, :] * halo_recv[1, 1]
    edge_row_sum = jnp.sum(halo_p[...].T, axis=0, keepdims=True)
    ext[0:1, :] = edge_row_sum
    ext[nb + 1 : nb + 2, :] = edge_row_sum

    here = ext[...]
    before = pltpu.roll(here, 1, 0)
    after = pltpu.roll(here, 7, 0)
    halfspan = (kwidth[0] - 1) // 2
    pooled = here
    for shift in range(1, (KERNEL_LIMIT - 1) // 2 + 1):
        ahead = pltpu.roll(jnp.where(lane8 >= shift, here, after), 128 - shift, 1)
        behind = pltpu.roll(jnp.where(lane8 < 128 - shift, here, before), shift, 1)
        wider = jnp.maximum(jnp.maximum(pooled, ahead), behind)
        pooled = jnp.where(shift <= halfspan, wider, pooled)
    sums = jnp.broadcast_to(jnp.sum(pooled, axis=1, keepdims=True), (8, 128))
    mine = (sub8 >= 1) & (sub8 <= nb)
    local = jnp.sum(jnp.where(mine & (lane8 == sub8 - 1), sums, 0.0), axis=0, keepdims=True)
    blocks_out[...] = local[:, 0:nb]
    placed = jnp.sum(jnp.where(mine & (lane8 == s * nb + sub8 - 1), sums, 0.0), axis=0, keepdims=True)
    blk_recv[s] = jnp.broadcast_to(placed, (8, 128))
    each_peer(lambda d: blk_copy(d).start())
    each_peer(lambda d: blk_copy(d).wait_recv())
    row = jnp.sum(blk_recv[...], axis=0)[0:1, :]
    by_lane = jnp.broadcast_to(row, (128, 128))
    by_sub = by_lane.T
    si = lax.broadcasted_iota(jnp.int32, (128, 128), 0)
    li = lax.broadcasted_iota(jnp.int32, (128, 128), 1)
    larger = (by_sub > by_lane) | ((by_sub == by_lane) & (si < li))
    rank = jnp.sum(larger.astype(jnp.float32), axis=0, keepdims=True)
    kept = jnp.sum(jnp.where(rank < keep[0].astype(jnp.float32), row, 0.0), axis=1, keepdims=True)
    frac_out[...] = kept / jnp.sum(row, axis=1, keepdims=True)

    for cp in started:
        cp.wait_send()
    each_peer(lambda d: stat_copy(d).wait_send())
    each_peer(lambda d: blk_copy(d).wait_send())


def solution(mesh):
    n_seq = mesh.shape["seq"]

    def local(hidden, gain, key_matrix, value_matrix, queries, window_len, kernel_width, kept_block_count):
        tok, feat = hidden.shape
        width, hd = key_matrix.shape
        nq = queries.shape[0] * queries.shape[1] // hd
        nb = tok // BLK
        freq = (500000.0 ** (-(np.arange(hd // 2) * 2.0) / hd)).astype(np.float32)
        freq = jnp.asarray(np.concatenate([freq, freq])[None, :])
        anyspace = pl.BlockSpec(memory_space=pl.ANY)
        vmem = pl.BlockSpec(memory_space=pltpu.VMEM)
        smem = pl.BlockSpec(memory_space=pltpu.SMEM)
        f32, bf16 = jnp.float32, jnp.bfloat16
        dma = pltpu.SemaphoreType.DMA
        blocks, frac = pl.pallas_call(
            functools.partial(kernel, n_seq),
            out_shape=(
                jax.ShapeDtypeStruct((1, nb), f32),
                jax.ShapeDtypeStruct((1, 1), f32),
            ),
            in_specs=[anyspace, vmem, anyspace, anyspace, vmem, smem, smem, smem, vmem],
            out_specs=(vmem, vmem),
            scratch_shapes=[
                pltpu.VMEM((8, tok, feat), bf16),
                pltpu.VMEM((width, 2 * hd), bf16),
                pltpu.VMEM((nq, hd), bf16),
                pltpu.VMEM((tok, hd), f32),
                pltpu.VMEM((tok, hd), f32),
                pltpu.VMEM((tok, 2 * hd), f32),
                pltpu.VMEM((tok, 128), f32),
                pltpu.VMEM((tok, 128), f32),
                pltpu.VMEM((tok, nq), f32),
                pltpu.VMEM((nb + 1, 8, 128), f32),
                pltpu.VMEM((nb + 1, 8, 128), f32),
                pltpu.VMEM((8, 128), f32),
                pltpu.VMEM((BLK, 128), f32),
                pltpu.VMEM((2, 2, 16, 128), f32),
                pltpu.VMEM((2, 2, 16, 128), f32),
                pltpu.VMEM((n_seq, 8, 128), f32),
                pltpu.VMEM((n_seq, 8, 128), f32),
                dma((3,)),
                dma((2, CHUNKS)),
                dma((CHUNKS,)),
                dma((CHUNKS,)),
                dma((3, CHUNKS)),
                dma((8, CHUNKS)),
                dma((2,)),
                dma((2,)),
                dma((n_seq,)),
                dma((n_seq,)),
                dma((n_seq,)),
                dma((n_seq,)),
            ],
            compiler_params=pltpu.CompilerParams(
                collective_id=0, has_side_effects=True, vmem_limit_bytes=56 * 1024 * 1024
            ),
        )(
            hidden, gain.reshape(1, -1), key_matrix, value_matrix, queries,
            window_len, kernel_width, kept_block_count, freq,
        )
        return blocks, frac.reshape(1)

    return jax.shard_map(
        local,
        mesh=mesh,
        in_specs=(
            P("seq", "head"), P(), P(None, "head"), P(None, "head"), P(None, "head"),
            P("head"), P("head"), P("head"),
        ),
        out_specs=(P("head", "seq"), P("head")),
        check_vma=False,
    )
```

time: 134 us -> 74.3 us (0.55); the launches traced: 132 us -> 74.2 us
  Pallas kernels: 0 us -> 68.7 us
  waiting for transfers between devices: 65.5 us -> 0 us
  starting transfers between devices: 29.1 us -> 0 us
  between operations: 18.7 us -> 4.34 us
  matrix products: 8.29 us -> 0 us
  other arithmetic: 6.1 us -> 0 us
  local copies, waits for them, and re-layouts: 3.82 us -> 1.11 us
    pallas_call x0 -> x1, Pallas kernels: none -> 68.7 us  [local(): pl.pallas_call(functools.partial(kernel, n_seq), out_shape=(jax.ShapeDtyp...]
    all_gather x1 -> x0, waiting for transfers between devices: 45.1 us -> none  [local(): lax.all_gather(hidden, 'head', axis=1, tiled=True).astype(jnp.float32)]
    all_to_all x3 -> x0, starting transfers between devices: 23.7 us -> none  [copy_for_each(): lax.all_to_all(jnp.broadcast_to(x[None], (count, *x.shape)), axis, 0, 0,...]
    all_to_all x3 -> x0, waiting for transfers between devices: 19.1 us -> none  [copy_for_each(): lax.all_to_all(jnp.broadcast_to(x[None], (count, *x.shape)), axis, 0, 0,...]
    dot_general x3 -> x0, matrix products: 8.29 us -> none  [the longest x1 6.96 us: local(): projected = jnp.dot(normed, joined, preferred_element_type=jnp.float32)]
    ppermute x2 -> x0, starting transfers between devices: 5.39 us -> none  [the longest x1 4.1 us: with_halo(): before = lax.ppermute(last, axis, up)]
    reduce_sum x6 -> x0, other arithmetic: 2.65 us -> none  [the longest x1 1.5 us: local(): sumsq = taken_together(jnp.sum(floats * floats, axis=1), 'head')]
    sort x1 -> x0, other arithmetic: 2.61 us -> none  [local(): ordered = -jnp.sort(-everything)]
  transfers between devices with their start and end apart: 6 -> 0, of which waited for: 5 -> 0; matrix products, arithmetic and copies ran while one was open for 3% -> 0% of each run, Pallas kernels for 0% -> 0%
where the time goes in v1:
time: 74.3 us; the launch traced here: 74.2 us
  Pallas kernels  68.7 us (92%)
  between operations  4.34 us (6%)
  local copies, waits for them, and re-layouts  1.11 us (1%)
    pallas_call x1, Pallas kernels, local(): pl.pallas_call(functools.partial(kernel, n_seq), out_shape=(jax.ShapeDtyp...  68.7 us

profile of v1, /device:TPU:1, one launch (start us, length us, event | category | flops | bytes accessed | tf_op | source)
XLA Modules:
  0.0 74.2 jit_solution(18353159991239620179)
XLA Ops:
  2.6 68.7 %shard_map.104 = (f32[1,4]{1,0:T(1,128)}, f32[1,1]{1,0:T(1,128)}) custom-call(bf16[512,1024]{1,0:T(8,128)(2,1)} %hid.1, f32[1,8192]{1,0:T(1,128)} %bitcast.2, bf16[8192,128]{1,0:T(8,128)(2,1)} %wk.1, bf16[8192,128]{1,0:T(8,128)(2,1)} %wv.1, bf16[64,1024]{1,0:T(8,128)(2,1)} %q.1, s32[1]{0:T(128)S(6)} %copy.13.wlen, s32[1]{0:T(128)S(6)} %copy.14.kwidth, ...), custom_call_target="tpu_custom_call" | custom-call | tf_op jit(solution)/shard_map/pallas_call | solution.py:337
  71.3 1.1 %copy.16 = f32[1,4]{1,0:T(1,128)} copy(f32[1,4]{1,0:T(1,128)} %get-tuple-element.8) | data formatting | bytes 32

commit v2 on v1

--- a/solution.py
+++ b/solution.py
@@ -12,18 +12,19 @@
 BLK = 128
 KERNEL_LIMIT = 15
 NX = 4
+N_Z = 8
 CHUNKS = 8
 NEG = -1e30
 
 
 def kernel(
     n_seq,
-    hid, gain, wk, wv, q, wlen, kwidth, keep, freq,
+    hid, gain, wk, wv, q, wlen_in, kwidth_in, keep_in, freq,
     blocks_out, frac_out,
     hbuf, w, qs, cos_t, sin_t, acc, ssq, vmag, ex, stat, gt, ext, halo_p,
-    halo_send, halo_recv, stat_recv, blk_recv,
+    halo_send, halo_recv, stat_recv, blk_recv, wlen, kwidth, keep,
     load_sem, own_send, fwd_send, d2d_own_send, d2d_send, recv_sem,
-    halo_ssem, halo_rsem, stat_ssem, stat_rsem, blk_ssem, blk_rsem,
+    halo_ssem, halo_rsem, stat_ssem, stat_rsem, blk_ssem, blk_rsem, met,
 ):
     tok = hid.shape[0]
     feat = hid.shape[1]
@@ -40,6 +41,9 @@
     s = lax.axis_index("seq")
     h = lax.axis_index("head")
     x, c = h // 2, lax.rem(h, 2)
+    n_z = N_Z
+    n_y = n_seq // N_Z
+    y, z = s // n_z, lax.rem(s, n_z)
     xr, xl, xo = lax.rem(x + 1, NX), lax.rem(x + 3, NX), lax.rem(x + 2, NX)
     right = {"seq": s, "head": xr * 2 + c}
     left = {"seq": s, "head": xl * 2 + c}
@@ -54,21 +58,39 @@
         pltpu.make_async_copy(hid, hbuf.at[0], load_sem.at[0]),
         pltpu.make_async_copy(wk, w.at[:, 0:hd], load_sem.at[1]),
         pltpu.make_async_copy(wv, w.at[:, hd : 2 * hd], load_sem.at[2]),
+        pltpu.make_async_copy(wlen_in, wlen, load_sem.at[3]),
+        pltpu.make_async_copy(kwidth_in, kwidth, load_sem.at[4]),
+        pltpu.make_async_copy(keep_in, keep, load_sem.at[5]),
     ]
     for cp in loads:
         cp.start()
 
+    ring = {
+        name: {"seq": at, "head": h}
+        for name, at in (
+            ("z+", y * n_z + lax.rem(z + 1, n_z)),
+            ("z-", y * n_z + lax.rem(z + n_z - 1, n_z)),
+            ("y+", lax.rem(y + 1, n_y) * n_z + z),
+            ("y-", lax.rem(y + n_y - 1, n_y) * n_z + z),
+        )
+    }
     barrier = pltpu.get_barrier_semaphore()
-    for dev in (right, left, partner):
+    for dev in (right, left, partner, *ring.values()):
         pl.semaphore_signal(barrier, inc=1, device_id=dev, device_id_type=MESH)
-
-    def greet(d, carry):
-        dev = {"seq": lax.rem(s + d, n_seq), "head": h}
-        pl.semaphore_signal(barrier, inc=1, device_id=dev, device_id_type=MESH)
-        return carry
-
-    lax.fori_loop(1, n_seq, greet, 0)
-    pl.semaphore_wait(barrier, 3 + n_seq - 1)
+    pl.semaphore_wait(barrier, 3 + len(ring))
+
+    rounds = ["z"] * (n_z // 2 - 1) + ["y"] * (n_y // 2)
+
+    def tell(r):
+        for side in "+-":
+            pl.semaphore_signal(met.at[r], inc=1, device_id=ring[rounds[r] + side], device_id_type=MESH)
+
+    def meet(r):
+        pl.semaphore_wait(met.at[r], 2)
+        if r + 1 < len(rounds):
+            tell(r + 1)
+
+    tell(0)
 
     def part(k):
         return slice(k * rows, (k + 1) * rows)
@@ -129,7 +151,9 @@
 
         lax.fori_loop(0, count, body, 0)
 
+    meet(0)
     accumulate(0, 0, nb, BLK, fresh=True)
+    meet(1)
     for k in range(CHUNKS):
         landed(4, k)
     accumulate(4, 0, nb, BLK)
@@ -152,6 +176,8 @@
             landed(6, k)
         accumulate(5, b * BLK, 1, BLK)
         accumulate(6, b * BLK, 1, BLK)
+        if 2 + b < len(rounds):
+            meet(2 + b)
 
     lane_q = lax.broadcasted_iota(jnp.int32, (1, nq), 1)
     limit = total_tokens - window + lax.rem(lane_q, window)
@@ -331,7 +357,6 @@
         freq = jnp.asarray(np.concatenate([freq, freq])[None, :])
         anyspace = pl.BlockSpec(memory_space=pl.ANY)
         vmem = pl.BlockSpec(memory_space=pltpu.VMEM)
-        smem = pl.BlockSpec(memory_space=pltpu.SMEM)
         f32, bf16 = jnp.float32, jnp.bfloat16
         dma = pltpu.SemaphoreType.DMA
         blocks, frac = pl.pallas_call(
@@ -340,7 +365,7 @@
                 jax.ShapeDtypeStruct((1, nb), f32),
                 jax.ShapeDtypeStruct((1, 1), f32),
             ),
-            in_specs=[anyspace, vmem, anyspace, anyspace, vmem, smem, smem, smem, vmem],
+            in_specs=[anyspace, vmem, anyspace, anyspace, vmem, anyspace, anyspace, anyspace, vmem],
             out_specs=(vmem, vmem),
             scratch_shapes=[
                 pltpu.VMEM((8, tok, feat), bf16),
@@ -360,7 +385,10 @@
                 pltpu.VMEM((2, 2, 16, 128), f32),
                 pltpu.VMEM((n_seq, 8, 128), f32),
                 pltpu.VMEM((n_seq, 8, 128), f32),
-                dma((3,)),
+                pltpu.SMEM((1,), jnp.int32),
+                pltpu.SMEM((1,), jnp.int32),
+                pltpu.SMEM((1,), jnp.int32),
+                dma((6,)),
                 dma((2, CHUNKS)),
                 dma((CHUNKS,)),
                 dma((CHUNKS,)),
@@ -372,6 +400,7 @@
                 dma((n_seq,)),
                 dma((n_seq,)),
                 dma((n_seq,)),
+                pltpu.SemaphoreType.REGULAR((N_Z // 2 - 1 + n_seq // N_Z // 2,)),
             ],
             compiler_params=pltpu.CompilerParams(
                 collective_id=0, has_side_effects=True, vmem_limit_bytes=56 * 1024 * 1024

time: 74.3 us -> 71.2 us (0.958)
  Pallas kernels: 68.7 us -> 65.6 us
    pallas_call x1, Pallas kernels: 68.7 us -> 65.6 us  [local(): pl.pallas_call(functools.partial(kernel, n_seq), out_shape=(jax.ShapeDtyp...]
where the time goes in v2:
time: 71.2 us; the launch traced here: 71.1 us
  Pallas kernels  65.6 us (92%)
  between operations  4.34 us (6%)
  local copies, waits for them, and re-layouts  1.11 us (2%)
    pallas_call x1, Pallas kernels, local(): pl.pallas_call(functools.partial(kernel, n_seq), out_shape=(jax.ShapeDtyp...  65.6 us

profile of v2, /device:TPU:1, one launch (start us, length us, event | category | flops | bytes accessed | tf_op | source)
XLA Modules:
  0.0 71.1 jit_solution(11110702189735728114)
XLA Ops:
  2.6 65.6 %shard_map.104 = (f32[1,4]{1,0:T(1,128)}, f32[1,1]{1,0:T(1,128)}) custom-call(bf16[512,1024]{1,0:T(8,128)(2,1)} %hid.1, f32[1,8192]{1,0:T(1,128)} %bitcast.2, bf16[8192,128]{1,0:T(8,128)(2,1)} %wk.1, bf16[8192,128]{1,0:T(8,128)(2,1)} %wv.1, bf16[64,1024]{1,0:T(8,128)(2,1)} %q.1, s32[1]{0:T(128)S(6)} %copy.13.wlen_in, s32[1]{0:T(128)S(6)} %copy.14.kwidth_in, ...), custom_call_target="tpu_custom_call" | custom-call | tf_op jit(solution)/shard_map/pallas_call | solution.py:362
  68.2 1.1 %copy.16 = f32[1,4]{1,0:T(1,128)} copy(f32[1,4]{1,0:T(1,128)} %get-tuple-element.8) | data formatting | bytes 32

commit v3 on v2

--- a/solution.py
+++ b/solution.py
@@ -19,23 +19,23 @@
 
 def kernel(
     n_seq,
-    hid, gain, wk, wv, q, wlen_in, kwidth_in, keep_in, freq,
-    blocks_out, frac_out,
-    hbuf, w, qs, cos_t, sin_t, acc, ssq, vmag, ex, stat, gt, ext, halo_p,
-    halo_send, halo_recv, stat_recv, blk_recv, wlen, kwidth, keep,
+    hid, gain_in, wk, wv, q_in, counts_in, freq_in,
+    out,
+    hbuf, w, gain, q, freq, qs, qs_t, cos_t, sin_t, acc, ssq, vmag, ex, stat, gt, ext, halo_p,
+    halo_send, halo_recv, stat_recv, blk_recv, counts,
     load_sem, own_send, fwd_send, d2d_own_send, d2d_send, recv_sem,
     halo_ssem, halo_rsem, stat_ssem, stat_rsem, blk_ssem, blk_rsem, met,
 ):
     tok = hid.shape[0]
     feat = hid.shape[1]
     hd = wk.shape[1]
-    window = q.shape[0]
-    group = q.shape[1] // hd
+    window = q_in.shape[0]
+    group = q_in.shape[1] // hd
     nq = window * group
     nb = tok // BLK
     rows = tok // CHUNKS
     half = CHUNKS // 2
-    full_width = gain.shape[1]
+    full_width = gain_in.shape[1]
     total_tokens = tok * n_seq
 
     s = lax.axis_index("seq")
@@ -54,17 +54,6 @@
     src = [x * 2 + c, xl * 2 + c, xr * 2 + c, xo * 2 + c]
     src += [x * 2 + 1 - c, xl * 2 + 1 - c, xr * 2 + 1 - c, xo * 2 + 1 - c]
 
-    loads = [
-        pltpu.make_async_copy(hid, hbuf.at[0], load_sem.at[0]),
-        pltpu.make_async_copy(wk, w.at[:, 0:hd], load_sem.at[1]),
-        pltpu.make_async_copy(wv, w.at[:, hd : 2 * hd], load_sem.at[2]),
-        pltpu.make_async_copy(wlen_in, wlen, load_sem.at[3]),
-        pltpu.make_async_copy(kwidth_in, kwidth, load_sem.at[4]),
-        pltpu.make_async_copy(keep_in, keep, load_sem.at[5]),
-    ]
-    for cp in loads:
-        cp.start()
-
     ring = {
         name: {"seq": at, "head": h}
         for name, at in (
@@ -77,6 +66,17 @@
     barrier = pltpu.get_barrier_semaphore()
     for dev in (right, left, partner, *ring.values()):
         pl.semaphore_signal(barrier, inc=1, device_id=dev, device_id_type=MESH)
+    loads = [
+        pltpu.make_async_copy(hid, hbuf.at[0], load_sem.at[0]),
+        pltpu.make_async_copy(wk, w.at[:, 0:hd], load_sem.at[1]),
+        pltpu.make_async_copy(wv, w.at[:, hd : 2 * hd], load_sem.at[2]),
+        pltpu.make_async_copy(counts_in, counts, load_sem.at[3]),
+        pltpu.make_async_copy(gain_in, gain, load_sem.at[4]),
+        pltpu.make_async_copy(q_in, q, load_sem.at[5]),
+        pltpu.make_async_copy(freq_in, freq, load_sem.at[6]),
+    ]
+    for cp in loads:
+        cp.start()
     pl.semaphore_wait(barrier, 3 + len(ring))
 
     rounds = ["z"] * (n_z // 2 - 1) + ["y"] * (n_y // 2)
@@ -116,6 +116,8 @@
     def landed(slot, k):
         send(hbuf.at[slot, part(k)], slot, k, own_send.at[0, 0], right).wait_recv()
 
+    for cp in loads:
+        cp.wait()
     for b in range(nb):
         position = (s * tok + b * BLK + lax.broadcasted_iota(jnp.int32, (BLK, hd), 0)).astype(jnp.float32)
         angle = position * freq[0:1, :]
@@ -125,8 +127,7 @@
         sin_t[b * BLK : (b + 1) * BLK, :] = jnp.where(lane < hd // 2, -sine, sine)
     for j in range(group):
         qs[j * window : (j + 1) * window, :] = q[:, j * hd : (j + 1) * hd]
-    for cp in loads:
-        cp.wait()
+    qs_t[...] = qs[...].astype(jnp.float32).T.astype(jnp.bfloat16)
 
     def accumulate(slot, first, count, size, fresh=False):
         head = src[slot]
@@ -183,9 +184,7 @@
     limit = total_tokens - window + lax.rem(lane_q, window)
 
     def scores_of(keys):
-        return lax.dot_general(
-            keys, qs[...], (((1,), (1,)), ((), ())), preferred_element_type=jnp.float32
-        ) * hd ** (-0.5)
+        return jnp.dot(keys, qs_t[...], preferred_element_type=jnp.float32) * hd ** (-0.5)
 
     def halo_copy(side, dev):
         return pltpu.make_async_remote_copy(
@@ -287,7 +286,7 @@
     sub8 = lax.broadcasted_iota(jnp.int32, (8, 128), 0)
     lane8 = lax.broadcasted_iota(jnp.int32, (8, 128), 1)
     wrow = lax.rem(lane8, window)
-    used = (wrow >= window - wlen[0]) & (sub8 < 4)
+    used = (wrow >= window - counts[0:1, 0:1]) & (sub8 < 4)
     for b in range(nb + 1):
         factor = jnp.exp(stat[b] - row_top) / row_total
         gt[b] = jnp.where(used, factor, 0.0)
@@ -314,7 +313,7 @@
     here = ext[...]
     before = pltpu.roll(here, 1, 0)
     after = pltpu.roll(here, 7, 0)
-    halfspan = (kwidth[0] - 1) // 2
+    halfspan = lax.shift_right_logical(counts[0:1, 1:2] - 1, 1)
     pooled = here
     for shift in range(1, (KERNEL_LIMIT - 1) // 2 + 1):
         ahead = pltpu.roll(jnp.where(lane8 >= shift, here, after), 128 - shift, 1)
@@ -324,7 +323,6 @@
     sums = jnp.broadcast_to(jnp.sum(pooled, axis=1, keepdims=True), (8, 128))
     mine = (sub8 >= 1) & (sub8 <= nb)
     local = jnp.sum(jnp.where(mine & (lane8 == sub8 - 1), sums, 0.0), axis=0, keepdims=True)
-    blocks_out[...] = local[:, 0:nb]
     placed = jnp.sum(jnp.where(mine & (lane8 == s * nb + sub8 - 1), sums, 0.0), axis=0, keepdims=True)
     blk_recv[s] = jnp.broadcast_to(placed, (8, 128))
     each_peer(lambda d: blk_copy(d).start())
@@ -336,13 +334,21 @@
     li = lax.broadcasted_iota(jnp.int32, (128, 128), 1)
     larger = (by_sub > by_lane) | ((by_sub == by_lane) & (si < li))
     rank = jnp.sum(larger.astype(jnp.float32), axis=0, keepdims=True)
-    kept = jnp.sum(jnp.where(rank < keep[0].astype(jnp.float32), row, 0.0), axis=1, keepdims=True)
-    frac_out[...] = kept / jnp.sum(row, axis=1, keepdims=True)
+    kept = jnp.sum(jnp.where(rank < counts[0:1, 2:3].astype(jnp.float32), row, 0.0), axis=1, keepdims=True)
+    fraction = kept / jnp.sum(row, axis=1, keepdims=True)
+    lane1 = lax.broadcasted_iota(jnp.int32, (1, 128), 1)
+    out[...] = jnp.where(lane1 < nb, local, fraction)
 
     for cp in started:
         cp.wait_send()
     each_peer(lambda d: stat_copy(d).wait_send())
     each_peer(lambda d: blk_copy(d).wait_send())
+
+
+def split_kernel(joined, blocks, frac):
+    nb = blocks.shape[1]
+    blocks[...] = joined[:, 0:nb]
+    frac[...] = joined[:, nb : nb + 1]
 
 
 def solution(mesh):
@@ -359,18 +365,22 @@
         vmem = pl.BlockSpec(memory_space=pltpu.VMEM)
         f32, bf16 = jnp.float32, jnp.bfloat16
         dma = pltpu.SemaphoreType.DMA
-        blocks, frac = pl.pallas_call(
+        lane = lax.broadcasted_iota(jnp.int32, (1, 128), 1)
+        row = lambda v: lax.broadcast_in_dim(v, (1, 128), (0,))
+        counts = jnp.where(lane == 0, row(window_len), jnp.where(lane == 1, row(kernel_width), row(kept_block_count)))
+        joined = pl.pallas_call(
             functools.partial(kernel, n_seq),
-            out_shape=(
-                jax.ShapeDtypeStruct((1, nb), f32),
-                jax.ShapeDtypeStruct((1, 1), f32),
-            ),
-            in_specs=[anyspace, vmem, anyspace, anyspace, vmem, anyspace, anyspace, anyspace, vmem],
-            out_specs=(vmem, vmem),
+            out_shape=jax.ShapeDtypeStruct((1, 128), f32),
+            in_specs=[anyspace] * 7,
+            out_specs=vmem,
             scratch_shapes=[
                 pltpu.VMEM((8, tok, feat), bf16),
                 pltpu.VMEM((width, 2 * hd), bf16),
+                pltpu.VMEM((1, width), f32),
+                pltpu.VMEM(queries.shape, bf16),
+                pltpu.VMEM((1, hd), f32),
                 pltpu.VMEM((nq, hd), bf16),
+                pltpu.VMEM((hd, nq), bf16),
                 pltpu.VMEM((tok, hd), f32),
                 pltpu.VMEM((tok, hd), f32),
                 pltpu.VMEM((tok, 2 * hd), f32),
@@ -385,10 +395,8 @@
                 pltpu.VMEM((2, 2, 16, 128), f32),
                 pltpu.VMEM((n_seq, 8, 128), f32),
                 pltpu.VMEM((n_seq, 8, 128), f32),
-                pltpu.SMEM((1,), jnp.int32),
-                pltpu.SMEM((1,), jnp.int32),
-                pltpu.SMEM((1,), jnp.int32),
-                dma((6,)),
+                pltpu.VMEM((1, 128), jnp.int32),
+                dma((7,)),
                 dma((2, CHUNKS)),
                 dma((CHUNKS,)),
                 dma((CHUNKS,)),
@@ -407,8 +415,14 @@
             ),
         )(
             hidden, gain.reshape(1, -1), key_matrix, value_matrix, queries,
-            window_len, kernel_width, kept_block_count, freq,
-        )
+            counts, freq,
+        )
+        blocks, frac = pl.pallas_call(
+            split_kernel,
+            out_shape=(jax.ShapeDtypeStruct((1, nb), f32), jax.ShapeDtypeStruct((1, 1), f32)),
+            in_specs=[vmem],
+            out_specs=(vmem, vmem),
+        )(joined)
         return blocks, frac.reshape(1)
 
     return jax.shard_map(

time: 71.2 us -> 69 us (0.969)
  between operations: 4.34 us -> 2.57 us
  local copies, waits for them, and re-layouts: 1.11 us -> 0 us
    unnamed x1 -> x0, local copies, waits for them, and re-layouts: 1.11 us -> none
    pallas_call x1 -> x2, Pallas kernels: 65.6 us -> 65.8 us  [the longest x1 64.6 us: local(): pl.pallas_call(functools.partial(kernel, n_seq), out_shape=jax.ShapeDtype...]
where the time goes in v3:
time: 69 us; the launch traced here: 68.9 us
  Pallas kernels  65.8 us (95%)
  between operations  2.57 us (4%)
    pallas_call x1, Pallas kernels, local(): pl.pallas_call(functools.partial(kernel, n_seq), out_shape=jax.ShapeDtype...  64.6 us

profile of v3, /device:TPU:1, one launch (start us, length us, event | category | flops | bytes accessed | tf_op | source)
XLA Modules:
  0.0 68.9 jit_solution(16844759200221707965)
XLA Ops:
  2.6 0.5 compare_select_fusion.1.counts_in
  3.1 64.6 %shard_map.113.joined = f32[1,128]{1,0:T(1,128)} custom-call(bf16[512,1024]{1,0:T(8,128)(2,1)} %hid.1, f32[1,8192]{1,0:T(1,128)} %bitcast.8, bf16[8192,128]{1,0:T(8,128)(2,1)} %wk.1, bf16[8192,128]{1,0:T(8,128)(2,1)} %wv.1, bf16[64,1024]{1,0:T(8,128)(2,1)} %q_in.1, s32[1,128]{1,0:T(1,128)} %compare_select_fusion.1.counts_in, f32[1,128]{1,0:T(1,128)} %constant.6.clone.freq_in), custom_call_target="tpu_custom_call" | custom-call | tf_op jit(solution)/shard_map/pallas_call | solution.py:371
  67.7 1.2 %shard_map.114 = (f32[1,4]{1,0:T(1,128)}, f32[1,1]{1,0:T(1,128)}) custom-call(f32[1,128]{1,0:T(1,128)} %shard_map.113.joined), custom_call_target="tpu_custom_call" | custom-call | tf_op jit(solution)/shard_map/pallas_call | solution.py:420

commit v4 on v3

--- a/solution.py
+++ b/solution.py
@@ -34,7 +34,6 @@
     nq = window * group
     nb = tok // BLK
     rows = tok // CHUNKS
-    half = CHUNKS // 2
     full_width = gain_in.shape[1]
     total_tokens = tok * n_seq
 
@@ -163,11 +162,11 @@
     for b in range(nb):
         for k in range(b * per, (b + 1) * per):
             landed(1, k)
-            if k < half:
+            if k % 2 == 0:
                 go(send(hbuf.at[1, part(k)], 3, k, fwd_send.at[k], right))
             go(send(hbuf.at[1, part(k)], 5, k, d2d_send.at[0, k], partner))
             landed(2, k)
-            if k >= half:
+            if k % 2 == 1:
                 go(send(hbuf.at[2, part(k)], 3, k, fwd_send.at[k], left))
             go(send(hbuf.at[2, part(k)], 6, k, d2d_send.at[1, k], partner))
         accumulate(1, b * BLK, 1, BLK)
@@ -221,19 +220,15 @@
             stat[b, j : j + 1, :] = top[:, j * 128 : (j + 1) * 128]
             stat[b, 4 + j : 5 + j, :] = tot[:, j * 128 : (j + 1) * 128]
 
-    for k in range(half):
-        landed(3, k)
-        go(send(hbuf.at[3, part(k)], 7, k, d2d_send.at[2, k], partner))
-        landed(3, half + k)
-        go(send(hbuf.at[3, part(half + k)], 7, half + k, d2d_send.at[2, half + k], partner))
-        if (k + 1) % per == 0:
-            i = k // per
-            for b in (i, nb // 2 + i):
-                accumulate(3, b * BLK, 1, BLK)
-                for m in range(b * per, (b + 1) * per):
-                    landed(7, m)
-                accumulate(7, b * BLK, 1, BLK)
-                finish(b)
+    for b in range(nb):
+        for k in range(b * per, (b + 1) * per):
+            landed(3, k)
+            go(send(hbuf.at[3, part(k)], 7, k, d2d_send.at[2, k], partner))
+        accumulate(3, b * BLK, 1, BLK)
+        for k in range(b * per, (b + 1) * per):
+            landed(7, k)
+        accumulate(7, b * BLK, 1, BLK)
+        finish(b)
 
     merged = stat[0]
     for b in range(1, nb):

time: 69 us -> 67.4 us (0.977)
  Pallas kernels: 65.8 us -> 64.2 us
    pallas_call x1, Pallas kernels: 64.6 us -> 63 us  [local(): pl.pallas_call(functools.partial(kernel, n_seq), out_shape=jax.ShapeDtype...]
where the time goes in v4:
time: 67.4 us; the launch traced here: 67.3 us
  Pallas kernels  64.2 us (95%)
  between operations  2.57 us (4%)
    pallas_call x1, Pallas kernels, local(): pl.pallas_call(functools.partial(kernel, n_seq), out_shape=jax.ShapeDtype...  63 us

profile of v4, /device:TPU:1, one launch (start us, length us, event | category | flops | bytes accessed | tf_op | source)
XLA Modules:
  0.0 67.3 jit_solution(5698892568007441841)
XLA Ops:
  2.6 0.5 compare_select_fusion.1.counts_in
  3.1 63.0 %shard_map.113.joined = f32[1,128]{1,0:T(1,128)} custom-call(bf16[512,1024]{1,0:T(8,128)(2,1)} %hid.1, f32[1,8192]{1,0:T(1,128)} %bitcast.8, bf16[8192,128]{1,0:T(8,128)(2,1)} %wk.1, bf16[8192,128]{1,0:T(8,128)(2,1)} %wv.1, bf16[64,1024]{1,0:T(8,128)(2,1)} %q_in.1, s32[1,128]{1,0:T(1,128)} %compare_select_fusion.1.counts_in, f32[1,128]{1,0:T(1,128)} %constant.6.clone.freq_in), custom_call_target="tpu_custom_call" | custom-call | tf_op jit(solution)/shard_map/pallas_call | solution.py:366
  66.1 1.2 %shard_map.114 = (f32[1,4]{1,0:T(1,128)}, f32[1,1]{1,0:T(1,128)}) custom-call(f32[1,128]{1,0:T(1,128)} %shard_map.113.joined), custom_call_target="tpu_custom_call" | custom-call | tf_op jit(solution)/shard_map/pallas_call | solution.py:415

commit v5 on v4

--- a/solution.py
+++ b/solution.py
@@ -14,15 +14,16 @@
 NX = 4
 N_Z = 8
 CHUNKS = 8
+OWN = 2
 NEG = -1e30
 
 
 def kernel(
     n_seq,
-    hid, gain_in, wk, wv, q_in, counts_in, freq_in,
+    hid, gain_in, wk, wv, q_in, wlen, kwidth, keep, freq_in,
     out,
     hbuf, w, gain, q, freq, qs, qs_t, cos_t, sin_t, acc, ssq, vmag, ex, stat, gt, ext, halo_p,
-    halo_send, halo_recv, stat_recv, blk_recv, counts,
+    halo_send, halo_recv, stat_recv, blk_recv,
     load_sem, own_send, fwd_send, d2d_own_send, d2d_send, recv_sem,
     halo_ssem, halo_rsem, stat_ssem, stat_rsem, blk_ssem, blk_rsem, met,
 ):
@@ -69,10 +70,9 @@
         pltpu.make_async_copy(hid, hbuf.at[0], load_sem.at[0]),
         pltpu.make_async_copy(wk, w.at[:, 0:hd], load_sem.at[1]),
         pltpu.make_async_copy(wv, w.at[:, hd : 2 * hd], load_sem.at[2]),
-        pltpu.make_async_copy(counts_in, counts, load_sem.at[3]),
-        pltpu.make_async_copy(gain_in, gain, load_sem.at[4]),
-        pltpu.make_async_copy(q_in, q, load_sem.at[5]),
-        pltpu.make_async_copy(freq_in, freq, load_sem.at[6]),
+        pltpu.make_async_copy(gain_in, gain, load_sem.at[3]),
+        pltpu.make_async_copy(q_in, q, load_sem.at[4]),
+        pltpu.make_async_copy(freq_in, freq, load_sem.at[5]),
     ]
     for cp in loads:
         cp.start()
@@ -91,12 +91,12 @@
 
     tell(0)
 
-    def part(k):
-        return slice(k * rows, (k + 1) * rows)
-
-    def send(source, slot, k, ssem, dev):
+    def part(k, n=CHUNKS):
+        return slice(k * (tok // n), (k + 1) * (tok // n))
+
+    def send(source, slot, k, ssem, dev, n=CHUNKS):
         return pltpu.make_async_remote_copy(
-            src_ref=source, dst_ref=hbuf.at[slot, part(k)], send_sem=ssem,
+            src_ref=source, dst_ref=hbuf.at[slot, part(k, n)], send_sem=ssem,
             recv_sem=recv_sem.at[slot, k], device_id=dev, device_id_type=MESH,
         )
 
@@ -106,14 +106,14 @@
         cp.start()
         started.append(cp)
 
-    for k in range(CHUNKS):
-        go(send(hid.at[part(k)], 1, k, own_send.at[0, k], right))
-        go(send(hid.at[part(k)], 2, k, own_send.at[1, k], left))
-    for k in range(CHUNKS):
-        go(send(hid.at[part(k)], 4, k, d2d_own_send.at[k], partner))
-
-    def landed(slot, k):
-        send(hbuf.at[slot, part(k)], slot, k, own_send.at[0, 0], right).wait_recv()
+    for k in range(OWN):
+        go(send(hid.at[part(k, OWN)], 1, k, own_send.at[0, k], right, OWN))
+        go(send(hid.at[part(k, OWN)], 2, k, own_send.at[1, k], left, OWN))
+    for k in range(OWN):
+        go(send(hid.at[part(k, OWN)], 4, k, d2d_own_send.at[k], partner, OWN))
+
+    def landed(slot, k, n=CHUNKS):
+        send(hbuf.at[slot, part(k, n)], slot, k, own_send.at[0, 0], right, n).wait_recv()
 
     for cp in loads:
         cp.wait()
@@ -154,30 +154,33 @@
     meet(0)
     accumulate(0, 0, nb, BLK, fresh=True)
     meet(1)
-    for k in range(CHUNKS):
-        landed(4, k)
+    for k in range(OWN):
+        landed(4, k, OWN)
     accumulate(4, 0, nb, BLK)
 
     per = BLK // rows
-    for b in range(nb):
-        for k in range(b * per, (b + 1) * per):
-            landed(1, k)
-            if k % 2 == 0:
-                go(send(hbuf.at[1, part(k)], 3, k, fwd_send.at[k], right))
-            go(send(hbuf.at[1, part(k)], 5, k, d2d_send.at[0, k], partner))
-            landed(2, k)
-            if k % 2 == 1:
-                go(send(hbuf.at[2, part(k)], 3, k, fwd_send.at[k], left))
-            go(send(hbuf.at[2, part(k)], 6, k, d2d_send.at[1, k], partner))
-        accumulate(1, b * BLK, 1, BLK)
-        accumulate(2, b * BLK, 1, BLK)
-        for k in range(b * per, (b + 1) * per):
-            landed(5, k)
-            landed(6, k)
-        accumulate(5, b * BLK, 1, BLK)
-        accumulate(6, b * BLK, 1, BLK)
-        if 2 + b < len(rounds):
-            meet(2 + b)
+    for k in range(OWN):
+        inside = range(k * CHUNKS // OWN, (k + 1) * CHUNKS // OWN)
+        batches = nb // OWN
+        landed(1, k, OWN)
+        for m in inside:
+            if m % 2 == 0:
+                go(send(hbuf.at[1, part(m)], 3, m, fwd_send.at[m], right))
+        go(send(hbuf.at[1, part(k, OWN)], 5, k, d2d_send.at[0, k], partner, OWN))
+        landed(2, k, OWN)
+        for m in inside:
+            if m % 2 == 1:
+                go(send(hbuf.at[2, part(m)], 3, m, fwd_send.at[m], left))
+        go(send(hbuf.at[2, part(k, OWN)], 6, k, d2d_send.at[1, k], partner, OWN))
+        accumulate(1, k * batches * BLK, batches, BLK)
+        accumulate(2, k * batches * BLK, batches, BLK)
+        landed(5, k, OWN)
+        landed(6, k, OWN)
+        accumulate(5, k * batches * BLK, batches, BLK)
+        accumulate(6, k * batches * BLK, batches, BLK)
+        meet(2 + k)
+    for r in range(2 + OWN, len(rounds)):
+        meet(r)
 
     lane_q = lax.broadcasted_iota(jnp.int32, (1, nq), 1)
     limit = total_tokens - window + lax.rem(lane_q, window)
@@ -247,7 +250,7 @@
 
     def blk_copy(d):
         return pltpu.make_async_remote_copy(
-            src_ref=blk_recv.at[s], dst_ref=blk_recv.at[s], send_sem=blk_ssem.at[d],
+            src_ref=blk_recv.at[s, 0:1], dst_ref=blk_recv.at[s, 0:1], send_sem=blk_ssem.at[d],
             recv_sem=blk_rsem.at[d], device_id={"seq": lax.rem(s + d, n_seq), "head": h}, device_id_type=MESH,
         )
 
@@ -281,7 +284,7 @@
     sub8 = lax.broadcasted_iota(jnp.int32, (8, 128), 0)
     lane8 = lax.broadcasted_iota(jnp.int32, (8, 128), 1)
     wrow = lax.rem(lane8, window)
-    used = (wrow >= window - counts[0:1, 0:1]) & (sub8 < 4)
+    used = (wrow >= window - wlen[0]) & (sub8 < 4)
     for b in range(nb + 1):
         factor = jnp.exp(stat[b] - row_top) / row_total
         gt[b] = jnp.where(used, factor, 0.0)
@@ -308,7 +311,7 @@
     here = ext[...]
     before = pltpu.roll(here, 1, 0)
     after = pltpu.roll(here, 7, 0)
-    halfspan = lax.shift_right_logical(counts[0:1, 1:2] - 1, 1)
+    halfspan = (kwidth[0] - 1) // 2
     pooled = here
     for shift in range(1, (KERNEL_LIMIT - 1) // 2 + 1):
         ahead = pltpu.roll(jnp.where(lane8 >= shift, here, after), 128 - shift, 1)
@@ -319,17 +322,17 @@
     mine = (sub8 >= 1) & (sub8 <= nb)
     local = jnp.sum(jnp.where(mine & (lane8 == sub8 - 1), sums, 0.0), axis=0, keepdims=True)
     placed = jnp.sum(jnp.where(mine & (lane8 == s * nb + sub8 - 1), sums, 0.0), axis=0, keepdims=True)
-    blk_recv[s] = jnp.broadcast_to(placed, (8, 128))
+    blk_recv[s, 0:1, :] = placed
     each_peer(lambda d: blk_copy(d).start())
     each_peer(lambda d: blk_copy(d).wait_recv())
-    row = jnp.sum(blk_recv[...], axis=0)[0:1, :]
+    row = jnp.sum(blk_recv[:, 0:1, :], axis=0)
     by_lane = jnp.broadcast_to(row, (128, 128))
     by_sub = by_lane.T
     si = lax.broadcasted_iota(jnp.int32, (128, 128), 0)
     li = lax.broadcasted_iota(jnp.int32, (128, 128), 1)
     larger = (by_sub > by_lane) | ((by_sub == by_lane) & (si < li))
     rank = jnp.sum(larger.astype(jnp.float32), axis=0, keepdims=True)
-    kept = jnp.sum(jnp.where(rank < counts[0:1, 2:3].astype(jnp.float32), row, 0.0), axis=1, keepdims=True)
+    kept = jnp.sum(jnp.where(rank < keep[0].astype(jnp.float32), row, 0.0), axis=1, keepdims=True)
     fraction = kept / jnp.sum(row, axis=1, keepdims=True)
     lane1 = lax.broadcasted_iota(jnp.int32, (1, 128), 1)
     out[...] = jnp.where(lane1 < nb, local, fraction)
@@ -358,15 +361,13 @@
         freq = jnp.asarray(np.concatenate([freq, freq])[None, :])
         anyspace = pl.BlockSpec(memory_space=pl.ANY)
         vmem = pl.BlockSpec(memory_space=pltpu.VMEM)
+        smem = pl.BlockSpec(memory_space=pltpu.SMEM)
         f32, bf16 = jnp.float32, jnp.bfloat16
         dma = pltpu.SemaphoreType.DMA
-        lane = lax.broadcasted_iota(jnp.int32, (1, 128), 1)
-        row = lambda v: lax.broadcast_in_dim(v, (1, 128), (0,))
-        counts = jnp.where(lane == 0, row(window_len), jnp.where(lane == 1, row(kernel_width), row(kept_block_count)))
         joined = pl.pallas_call(
             functools.partial(kernel, n_seq),
             out_shape=jax.ShapeDtypeStruct((1, 128), f32),
-            in_specs=[anyspace] * 7,
+            in_specs=[anyspace] * 5 + [smem] * 3 + [anyspace],
             out_specs=vmem,
             scratch_shapes=[
                 pltpu.VMEM((8, tok, feat), bf16),
@@ -390,8 +391,7 @@
                 pltpu.VMEM((2, 2, 16, 128), f32),
                 pltpu.VMEM((n_seq, 8, 128), f32),
                 pltpu.VMEM((n_seq, 8, 128), f32),
-                pltpu.VMEM((1, 128), jnp.int32),
-                dma((7,)),
+                dma((6,)),
                 dma((2, CHUNKS)),
                 dma((CHUNKS,)),
                 dma((CHUNKS,)),
@@ -410,7 +410,7 @@
             ),
         )(
             hidden, gain.reshape(1, -1), key_matrix, value_matrix, queries,
-            counts, freq,
+            window_len, kernel_width, kept_block_count, freq,
         )
         blocks, frac = pl.pallas_call(
             split_kernel,

time: 67.4 us -> 66.5 us (0.987)
  no operation moved by 1% of the time
where the time goes in v5:
time: 66.5 us; the launch traced here: 66.4 us
  Pallas kernels  63.8 us (96%)
  between operations  2.58 us (4%)
    pallas_call x1, Pallas kernels, local(): pl.pallas_call(functools.partial(kernel, n_seq), out_shape=jax.ShapeDtype...  62.7 us

profile of v5, /device:TPU:1, one launch (start us, length us, event | category | flops | bytes accessed | tf_op | source)
XLA Modules:
  0.0 66.4 jit_solution(16597041724597962604)
XLA Ops:
  2.6 62.7 %shard_map.104.joined = f32[1,128]{1,0:T(1,128)} custom-call(bf16[512,1024]{1,0:T(8,128)(2,1)} %hid.1, f32[1,8192]{1,0:T(1,128)} %bitcast.2, bf16[8192,128]{1,0:T(8,128)(2,1)} %wk.1, bf16[8192,128]{1,0:T(8,128)(2,1)} %wv.1, bf16[64,1024]{1,0:T(8,128)(2,1)} %q_in.1, s32[1]{0:T(128)S(6)} %copy.11.wlen, s32[1]{0:T(128)S(6)} %copy.12.kwidth, s32[1]{0:T(128)S(6)} %copy.13.keep, ...), custom_call_target="tpu_custom_call" | custom-call | tf_op jit(solution)/shard_map/pallas_call | solution.py:367
  65.2 1.2 %shard_map.105 = (f32[1,4]{1,0:T(1,128)}, f32[1,1]{1,0:T(1,128)}) custom-call(f32[1,128]{1,0:T(1,128)} %shard_map.104.joined), custom_call_target="tpu_custom_call" | custom-call | tf_op jit(solution)/shard_map/pallas_call | solution.py:415

commit v6 on v5

--- a/solution.py
+++ b/solution.py
@@ -242,24 +242,30 @@
         merged = jnp.where(sub < 4, top, scaled)
     stat_recv[s] = merged
 
+    def peer(d):
+        return {"seq": lax.rem(y + d // n_z, n_y) * n_z + lax.rem(z + d % n_z, n_z), "head": h}
+
     def stat_copy(d):
         return pltpu.make_async_remote_copy(
             src_ref=stat_recv.at[s], dst_ref=stat_recv.at[s], send_sem=stat_ssem.at[d],
-            recv_sem=stat_rsem.at[d], device_id={"seq": lax.rem(s + d, n_seq), "head": h}, device_id_type=MESH,
+            recv_sem=stat_rsem.at[d], device_id=peer(d), device_id_type=MESH,
         )
 
     def blk_copy(d):
         return pltpu.make_async_remote_copy(
             src_ref=blk_recv.at[s, 0:1], dst_ref=blk_recv.at[s, 0:1], send_sem=blk_ssem.at[d],
-            recv_sem=blk_rsem.at[d], device_id={"seq": lax.rem(s + d, n_seq), "head": h}, device_id_type=MESH,
-        )
+            recv_sem=blk_rsem.at[d], device_id=peer(d), device_id_type=MESH,
+        )
+
+    def distance(d):
+        dy, dz = d // n_z, d % n_z
+        return min(dy, n_y - dy) + min(dz, n_z - dz)
+
+    peers = sorted(range(1, n_seq), key=lambda d: (-distance(d), d))
 
     def each_peer(act):
-        def body(d, carry):
+        for d in peers:
             act(d)
-            return carry
-
-        lax.fori_loop(1, n_seq, body, 0)
 
     each_peer(lambda d: stat_copy(d).start())
 

time: 66.5 us -> 65.7 us (0.988)
  Pallas kernels: 63.8 us -> 63 us
    pallas_call x1, Pallas kernels: 62.7 us -> 61.8 us  [local(): pl.pallas_call(functools.partial(kernel, n_seq), out_shape=jax.ShapeDtype...]
where the time goes in v6:
time: 65.7 us; the launch traced here: 65.6 us
  Pallas kernels  63 us (96%)
  between operations  2.58 us (4%)
    pallas_call x1, Pallas kernels, local(): pl.pallas_call(functools.partial(kernel, n_seq), out_shape=jax.ShapeDtype...  61.8 us

profile of v6, /device:TPU:1, one launch (start us, length us, event | category | flops | bytes accessed | tf_op | source)
XLA Modules:
  0.0 65.6 jit_solution(9242149169930966859)
XLA Ops:
  2.6 61.8 %shard_map.104.joined = f32[1,128]{1,0:T(1,128)} custom-call(bf16[512,1024]{1,0:T(8,128)(2,1)} %hid.1, f32[1,8192]{1,0:T(1,128)} %bitcast.2, bf16[8192,128]{1,0:T(8,128)(2,1)} %wk.1, bf16[8192,128]{1,0:T(8,128)(2,1)} %wv.1, bf16[64,1024]{1,0:T(8,128)(2,1)} %q_in.1, s32[1]{0:T(128)S(6)} %copy.11.wlen, s32[1]{0:T(128)S(6)} %copy.12.kwidth, s32[1]{0:T(128)S(6)} %copy.13.keep, ...), custom_call_target="tpu_custom_call" | custom-call | tf_op jit(solution)/shard_map/pallas_call | solution.py:373
  64.4 1.2 %shard_map.105 = (f32[1,4]{1,0:T(1,128)}, f32[1,1]{1,0:T(1,128)}) custom-call(f32[1,128]{1,0:T(1,128)} %shard_map.104.joined), custom_call_target="tpu_custom_call" | custom-call | tf_op jit(solution)/shard_map/pallas_call | solution.py:421

commit v7 on v6

--- a/solution.py
+++ b/solution.py
@@ -74,8 +74,6 @@
         pltpu.make_async_copy(q_in, q, load_sem.at[4]),
         pltpu.make_async_copy(freq_in, freq, load_sem.at[5]),
     ]
-    for cp in loads:
-        cp.start()
     pl.semaphore_wait(barrier, 3 + len(ring))
 
     rounds = ["z"] * (n_z // 2 - 1) + ["y"] * (n_y // 2)
@@ -88,8 +86,6 @@
         pl.semaphore_wait(met.at[r], 2)
         if r + 1 < len(rounds):
             tell(r + 1)
-
-    tell(0)
 
     def part(k, n=CHUNKS):
         return slice(k * (tok // n), (k + 1) * (tok // n))
@@ -111,6 +107,10 @@
         go(send(hid.at[part(k, OWN)], 2, k, own_send.at[1, k], left, OWN))
     for k in range(OWN):
         go(send(hid.at[part(k, OWN)], 4, k, d2d_own_send.at[k], partner, OWN))
+
+    for cp in loads:
+        cp.start()
+    tell(0)
 
     def landed(slot, k, n=CHUNKS):
         send(hbuf.at[slot, part(k, n)], slot, k, own_send.at[0, 0], right, n).wait_recv()
@@ -282,6 +282,8 @@
     for j in range(nq // 128):
         stat[nb, j : j + 1, :] = edge_top[:, j * 128 : (j + 1) * 128]
 
+    ext[...] = jnp.zeros_like(ext)
+    halo_p[...] = jnp.zeros_like(halo_p)
     each_peer(lambda d: stat_copy(d).wait_recv())
     everyone = stat_recv[...]
     row_top = jnp.max(everyone, axis=0)
@@ -301,13 +303,11 @@
             total = total + expo[:, j * 128 : (j + 1) * 128] * gt[b, j : j + 1, :]
         return total
 
-    ext[...] = jnp.zeros_like(ext)
     for b in range(nb):
         at = slice(b * BLK, (b + 1) * BLK)
         column = weighted(ex[at, :], b) * vmag[at, :]
         ext[b + 1 : b + 2, :] = jnp.sum(column.T, axis=0, keepdims=True)
     edge = weighted(edge_expo, nb)
-    halo_p[...] = jnp.zeros_like(halo_p)
     halo_p[0:16, :] = edge[0:16, :] * halo_recv[0, 1]
     halo_p[BLK - 16 :, :] = edge[16:32, :] * halo_recv[1, 1]
     edge_row_sum = jnp.sum(halo_p[...].T, axis=0, keepdims=True)

time: 65.7 us -> 65.7 us (level)
  no operation moved by 1% of the time
where the time goes in v7:
time: 65.7 us; the launch traced here: 65.6 us
  Pallas kernels  63 us (96%)
  between operations  2.58 us (4%)
    pallas_call x1, Pallas kernels, local(): pl.pallas_call(functools.partial(kernel, n_seq), out_shape=jax.ShapeDtype...  61.8 us

profile of v7, /device:TPU:1, one launch (start us, length us, event | category | flops | bytes accessed | tf_op | source)
XLA Modules:
  0.0 65.6 jit_solution(16678569188705763595)
XLA Ops:
  2.6 61.8 %shard_map.104.joined = f32[1,128]{1,0:T(1,128)} custom-call(bf16[512,1024]{1,0:T(8,128)(2,1)} %hid.1, f32[1,8192]{1,0:T(1,128)} %bitcast.2, bf16[8192,128]{1,0:T(8,128)(2,1)} %wk.1, bf16[8192,128]{1,0:T(8,128)(2,1)} %wv.1, bf16[64,1024]{1,0:T(8,128)(2,1)} %q_in.1, s32[1]{0:T(128)S(6)} %copy.11.wlen, s32[1]{0:T(128)S(6)} %copy.12.kwidth, s32[1]{0:T(128)S(6)} %copy.13.keep, ...), custom_call_target="tpu_custom_call" | custom-call | tf_op jit(solution)/shard_map/pallas_call | solution.py:373
  64.4 1.2 %shard_map.105 = (f32[1,4]{1,0:T(1,128)}, f32[1,1]{1,0:T(1,128)}) custom-call(f32[1,128]{1,0:T(1,128)} %shard_map.104.joined), custom_call_target="tpu_custom_call" | custom-call | tf_op jit(solution)/shard_map/pallas_call | solution.py:421
